TPU v7x, 128 devices: a whole 4x4x4 slice. The times are simulated.
128 devices in a mesh: blk: 32 (over z, x_lo, y), grp: 4 (over x_hi, core).
Axes of the slice: x: 4 (x_hi: 2, x_lo: 2; x = x_hi * 2 + x_lo), y: 4, z: 4, core: 2. Of those that a mesh axis runs over, the one named last changes fastest.
Arguments:
- acts: bfloat16 [1, 512, 256, 4096], P(None, 'blk', 'grp'), may hold values from -6 to 6
- out_grads: bfloat16 [1, 512, 256, 4096], P(None, 'blk', 'grp'), may hold values from -6 to 6
- proj_in: bfloat16 [1, 4096, 64], replicated, may hold values from -0.09375 to 0.09375
- proj_out: bfloat16 [1, 4096, 64], replicated, may hold values from -0.09375 to 0.09375
- lengths: int32 [512], P('blk'), may hold values from 1 to 256
- queries: bfloat16 [2048, 4096], P('blk'), may hold values from -0.09375 to 0.09375
Outputs:
- scores: float32 [512, 2048], P(('blk', 'grp'))
All inputs are finite; a program needn't handle non-finite values.
Results may differ from a plain program's by a relative error of at most 0.0049.
Values may be sent and summed in bfloat16 or wider, within the bound.
A program may use at most 128 MiB of HBM per device.

v0:
```python
import jax
import jax.numpy as jnp
from jax import lax
from jax.sharding import PartitionSpec as P


def project(rows, matrix):
    return jnp.einsum("lctd,ldr->lctr", rows, matrix, preferred_element_type=jnp.float32).astype(
        jnp.bfloat16
    )


def outer_sums(grad_side, input_side, lens):
    positions = jnp.arange(grad_side.shape[2], dtype=jnp.int32)
    masked = (positions[None, :] < lens[:, None]).astype(jnp.bfloat16)
    grad_masked = grad_side * masked[None, :, :, None]
    block = jnp.einsum(
        "lcta,lctb->clab", grad_masked, input_side, preferred_element_type=jnp.float32
    )
    return block.reshape(block.shape[0], -1)


def on_device(acts, out_grads, proj_in, proj_out, lengths, queries):
    group = lax.axis_index("grp")
    groups = lax.axis_size("grp")
    cand_blk = acts.shape[1]
    owned = cand_blk // groups
    stacked = jnp.concatenate([project(out_grads, proj_out), project(acts, proj_in)], axis=3)
    stacked = lax.all_to_all(stacked, "grp", split_axis=1, concat_axis=2, tiled=True)
    width = proj_in.shape[2]
    own_lens = lax.dynamic_slice_in_dim(lengths, group * owned, owned)
    grads = outer_sums(stacked[..., :width], stacked[..., width:], own_lens)
    scale = lax.rsqrt(jnp.mean(grads * grads, axis=1, keepdims=True) + 1e-06)
    unit = (grads * scale).astype(jnp.bfloat16)
    return lax.dot_general(
        unit,
        lax.all_gather(queries, "blk", axis=0, tiled=True),
        (((1,), (1,)), ((), ())),
        preferred_element_type=jnp.float32,
    )


def solution(mesh):
    in_specs = (
        P(None, "blk", "grp", None),
        P(None, "blk", "grp", None),
        P(),
        P(),
        P("blk"),
        P("blk", None),
    )
    out_specs = P(("blk", "grp"), None)
    return jax.shard_map(
        on_device, mesh=mesh, in_specs=in_specs, out_specs=out_specs, check_vma=False
    )
```

profile of v0, /device:TPU:0, one launch (start us, length us, event | category | flops | bytes accessed | tf_op | source)
XLA Modules:
  0.0 225.3 jit_solution(2176710123652143649)
XLA Ops:
  6.5 0.0 copy-start
  6.5 0.0 copy-start.2
  6.5 0.0 all-gather.2.cloned.1.call-start
  6.5 0.7 all-gather.2.cloned.1.call-update
  7.3 0.3 copy-done
  7.6 0.0 copy-start.1
  7.6 5.8 %fusion.10 = bf16[1,16,64,64]{3,2,1,0:T(8,128)(2,1)S(1)} fusion(bf16[1,16,64,4096]{3,2,1,0:T(8,128)(2,1)} %param.6, bf16[1,4096,64]{1,2,0:T(8,128)(2,1)S(1)} %copy-done), kind=kOutput, calls=%fused_computation.6 | convolution fusion | flops 536936448 | bytes 9043968 | tf_op jit(solution)/shard_map/lctd,ldr->lctr/dot_general | solution.py:8
  13.4 0.0 copy-done.2
  13.4 0.0 copy-done.1
  13.5 0.0 copy-start.3
  13.5 2.4 %fusion.13 = bf16[1,16,64,64]{3,2,1,0:T(8,128)(2,1)S(1)} fusion(bf16[1,16,64,4096]{3,2,1,0:T(8,128)(2,1)S(1)} %copy-done.1, bf16[1,4096,64]{1,2,0:T(8,128)(2,1)S(1)} %copy-done.2), kind=kOutput, calls=%fused_computation.7 | convolution fusion | flops 536936448 | bytes 9043968 | tf_op jit(solution)/shard_map/lctd,ldr->lctr/dot_general | solution.py:8
  15.8 0.9 maximum_bitcast_fusion
  16.7 4.4 %all-to-all-start = ((bf16[1,16,64,128]{3,2,0,1:T(8,128)(2,1)}), bf16[1,16,64,128]{3,2,0,1:T(8,128)(2,1)S(1)}, u32[]{:S(2)}, u32[]{:S(2)}) async-start(bf16[1,16,64,128]{3,2,0,1:T(8,128)(2,1)} %maximum_bitcast_fusion), calls=%async_computation | async-start | bytes 524288 | tf_op jit(solution)/shard_map/all_to_all | solution.py:29
  21.0 0.0 copy-done.3
  21.0 0.1 dynamic_slice.3
  21.1 0.1 fusion.24
  21.2 10.5 %all-to-all-done = bf16[1,16,64,128]{3,2,0,1:T(8,128)(2,1)S(1)} async-done(((bf16[1,16,64,128]{3,2,0,1:T(8,128)(2,1)}), bf16[1,16,64,128]{3,2,0,1:T(8,128)(2,1)S(1)}, u32[]{:S(2)}, u32[]{:S(2)}) %all-to-all-start) | async-done | bytes 262176 | tf_op jit(solution)/shard_map/all_to_all | solution.py:29
  31.7 0.6 multiply_reduce_fusion
  32.3 0.1 reshape.65
  32.4 175.2 %all-gather.2.cloned.1.call-done = bf16[2048,4096]{1,0:T(8,128)(2,1)} async-done(((bf16[64,4096]{1,0:T(8,128)(2,1)}), bf16[2048,4096]{1,0:T(8,128)(2,1)}) %all-gather.2.cloned.1.call-update) | async-done | bytes 16777232 | tf_op jit(solution)/shard_map/all_gather | solution.py:37
  207.6 10.8 %fusion.22 = f32[4,2048]{1,0:T(4,128)} fusion(bf16[2048,4096]{1,0:T(8,128)(2,1)} %all-gather.2.cloned.1.call-done, f32[4,4096]{1,0:T(4,128)S(1)} %reshape.65, f32[4]{0:T(128)S(1)} %add_rsqrt_fusion), kind=kOutput, calls=%fused_computation.18 | convolution fusion | flops 67141632 | bytes 16875536 | tf_op jit(solution)/shard_map/dot_general | solution.py:35
  (2 shorter events, 0.0 us)
Async XLA Ops:
  6.5 1.0 copy-start
  6.5 6.9 %copy-start.2 = (bf16[1,4096,64]{1,2,0:T(8,128)(2,1)S(1)}, bf16[1,4096,64]{1,2,0:T(8,128)(2,1)}, u32[]{:S(2)}) copy-start(bf16[1,4096,64]{1,2,0:T(8,128)(2,1)} %param.9) | copy-start | bytes 1572868
  6.5 201.1 %all-gather.2.cloned.1.call-start = ((), (), s32[]{:S(2)}) async-start(), calls=%async_computation.1 | async-start | bytes 17301504 | tf_op jit(solution)/shard_map/all_gather | solution.py:37
  7.6 5.9 %copy-start.1 = (bf16[1,16,64,4096]{3,2,1,0:T(8,128)(2,1)S(1)}, bf16[1,16,64,4096]{3,2,1,0:T(8,128)(2,1)}, u32[]{:S(2)}) copy-start(bf16[1,16,64,4096]{3,2,1,0:T(8,128)(2,1)} %param.7) | copy-start | bytes 25165828
  13.5 7.6 %copy-start.3 = (s32[16]{0:T(128)S(1)}, s32[16]{0:T(128)}, u32[]{:S(2)}) copy-start(s32[16]{0:T(128)} %param.10) | copy-start | bytes 196
  16.7 15.0 %all-to-all-start = ((bf16[1,16,64,128]{3,2,0,1:T(8,128)(2,1)}), bf16[1,16,64,128]{3,2,0,1:T(8,128)(2,1)S(1)}, u32[]{:S(2)}, u32[]{:S(2)}) async-start(bf16[1,16,64,128]{3,2,0,1:T(8,128)(2,1)} %maximum_bitcast_fusion), calls=%async_computation | async-start | bytes 524288 | tf_op jit(solution)/shard_map/all_to_all | solution.py:29
Sparse Core Ops, SparseCore 0:
  9.0 198.5 all-gather.1
where the time goes:
time: 226 us; the launch traced here: 225 us
  waiting for transfers between devices  186 us (82%)
  matrix products  19.6 us (9%)
  between operations  13.4 us (6%)
  starting transfers between devices  4.37 us (2%)
    all_gather x1, waiting for transfers between devices, on_device(): lax.all_gather(queries, 'blk', axis=0, tiled=True)  175 us
    dot_general x1, matrix products, on_device(): lax.dot_general(unit, lax.all_gather(queries, 'blk', axis=0, tiled=True),...  10.8 us
    all_to_all x1, waiting for transfers between devices, on_device(): lax.all_to_all(stacked, 'grp', split_axis=1, concat_axis=2, tiled=True)  10.5 us
    dot_general x2, matrix products, project(): jnp.einsum('lctd,ldr->lctr', rows, matrix, preferred_element_type=jnp.flo...  8.2 us
  transfers between devices with their start and end apart: 2, of which 2 were waited for; matrix products, arithmetic and copies ran while one was open for 4% of the time, Pallas kernels for 0%

commit v1 on v0

v1 whole, which is shorter than its diff:
```python
import functools

import jax
import jax.numpy as jnp
from jax import lax
from jax.experimental import pallas as pl
from jax.experimental.pallas import tpu as pltpu
from jax.sharding import PartitionSpec as P

MESH = pl.DeviceIdType.MESH
BF16, F32 = jnp.bfloat16, jnp.float32
D, PR, TOK = 4096, 64, 64
NT = (((1,), (1,)), ((), ()))
TN = (((0,), (0,)), ((), ()))
CHUNKS, AHEAD = 8, 2


def kernel(lens, acts, og, wi, wo, q, out,
           abuf, gbuf, wib, wob, pscr, pown, psend, pbuf, usend, ubuf, uf, qbuf, ssend, sbuf,
           ld_sem, w_sem, q_ssem, q_rsem, c_ssem, c_rsem, e_ssem, e_rsem, s_ssem, s_rsem):
    b, g = lax.axis_index("blk"), lax.axis_index("grp")
    z, xl, y = b // 8, (b // 4) % 2, b % 4
    xh, core = g // 2, g % 2

    def dev(z_, xl_, y_, xh_, c_):
        return (z_ * 8 + xl_ * 4 + y_, xh_ * 2 + c_)

    up, down = (y + 1) % 4, (y + 3) % 4
    y_up, y_down = dev(z, xl, up, xh, core), dev(z, xl, down, xh, core)
    x_up = dev(z, 1 - xl, y, (xh + xl) % 2, core)
    x_down = dev(z, 1 - xl, y, (xh + 1 - xl) % 2, core)
    z_peers = [((z + dz) % 4, (core + dc) % 2) for dz, dc in
               ((2, 0), (2, 1), (1, 0), (3, 0), (1, 1), (3, 1), (0, 1))]

    def target(s):
        return (xh + 1 - s // 2) % 2, (core + (s + 1) // 2) % 2

    barrier = pltpu.get_barrier_semaphore()
    partners = [y_up, y_down, x_up, x_down]
    partners += [dev(z_, xl, y, xh, c_) for z_, c_ in z_peers]
    partners += [dev(z, xl, y, *target(s)) for s in range(2)]
    for p in partners:
        pl.semaphore_signal(barrier, inc=1, device_id=p, device_id_type=MESH)

    def load(k):
        xt, ct = target(k // 2)
        first = (xt * 2 + ct) * 4 + (k % 2) * 2
        src = pl.ds(first, 2)
        return (pltpu.make_async_copy(acts.at[src], abuf.at[pl.ds(2 * k, 2)], ld_sem.at[k, 0]),
                pltpu.make_async_copy(og.at[src], gbuf.at[pl.ds(2 * k, 2)], ld_sem.at[k, 1]))

    own = xl * 4 + y
    w_loads = [pltpu.make_async_copy(wi, wib, w_sem.at[0]),
               pltpu.make_async_copy(wo, wob, w_sem.at[1])]
    q_load = pltpu.make_async_copy(
        q.at[:, pl.ds(pl.multiple_of(core * 2048, 2048), 2048)], qbuf.at[own], w_sem.at[2])
    for c in w_loads:
        c.start()
    for k in range(AHEAD):
        for c in load(k):
            c.start()
    q_load.start()

    def piece(slot, h):
        return qbuf.at[slot, pl.ds(h * 32, 32)]

    q_sends = []

    def send_q(slot, h, to):
        c = pltpu.make_async_remote_copy(
            src_ref=piece(slot, h), dst_ref=piece(slot, h), send_sem=q_ssem.at[len(q_sends)],
            recv_sem=q_rsem.at[slot, h], device_id=to, device_id_type=MESH)
        c.start()
        q_sends.append((slot, h, to))

    def wait_q(slot, h):
        pltpu.make_async_remote_copy(
            src_ref=piece(slot, h), dst_ref=piece(slot, h), send_sem=q_ssem.at[0],
            recv_sem=q_rsem.at[slot, h], device_id=y_up, device_id_type=MESH).wait_recv()

    near_up, near_down, far = xl * 4 + up, xl * 4 + down, xl * 4 + (y + 2) % 4
    q_load.wait()
    pl.semaphore_wait(barrier, len(partners))
    send_q(own, 0, y_up)
    send_q(own, 1, y_down)
    send_q(own, 0, x_up)
    send_q(own, 1, x_down)
    send_q(own, 1, y_up)
    send_q(own, 0, y_down)

    for c in w_loads:
        c.wait()
    pos = lax.broadcasted_iota(jnp.int32, (TOK, PR), 0) + g * TOK

    def chunk(k):
        for c in load(k):
            c.wait()

        @pl.when(k + AHEAD < CHUNKS)
        def _():
            for c in load(k + AHEAD):
                c.start()

        s = k // 2
        xt, ct = target(s)
        first = (xt * 2 + ct) * 4 + (k % 2) * 2
        x = abuf[pl.ds(2 * k, 2)].reshape(2 * TOK, D)
        gr = gbuf[pl.ds(2 * k, 2)].reshape(2 * TOK, D)
        xp = lax.dot_general(x, wib[...], NT, preferred_element_type=F32).astype(BF16)
        gp = lax.dot_general(gr, wob[...], NT, preferred_element_type=F32)
        for i in range(2):
            rows = slice(i * TOK, (i + 1) * TOK)
            masked = jnp.where(pos < lens[first + i], gp[rows], 0.0).astype(BF16)
            pscr[i] = lax.dot_general(masked, xp[rows], TN, preferred_element_type=F32)
            part = jnp.concatenate(
                [pscr[i, pl.ds(0, 32, stride=2), :], pscr[i, pl.ds(1, 32, stride=2), :]], axis=1)
            pown[(k % 2) * 2 + i] = part
            psend[s, (k % 2) * 2 + i] = part.astype(BF16)

    def send_part(s):
        return pltpu.make_async_remote_copy(
            src_ref=psend.at[s], dst_ref=pbuf.at[g], send_sem=c_ssem.at[s], recv_sem=c_rsem.at[g],
            device_id=dev(z, xl, y, *target(s)), device_id_type=MESH)

    def run(first, last):
        def body(k, carry):
            chunk(k)
            return carry
        lax.fori_loop(first, last, body, 0)

    run(0, 2)
    send_part(0).start()
    run(2, 4)
    send_part(1).start()
    wait_q(near_down, 0)
    send_q(near_down, 0, y_up)
    send_q(near_down, 0, x_up)
    wait_q(near_up, 1)
    send_q(near_up, 1, y_down)
    send_q(near_up, 1, x_down)
    run(4, 6)
    send_part(2).start()
    wait_q(near_down, 1)
    send_q(near_down, 1, x_down)
    wait_q(near_up, 0)
    send_q(near_up, 0, x_up)
    run(6, 8)
    wait_q(far, 0)
    send_q(far, 0, x_up)
    wait_q(far, 1)
    send_q(far, 1, x_down)

    total = pown[...]
    for s in range(3):
        xt, ct = target(s)
        src = xt * 2 + ct
        pltpu.make_async_remote_copy(
            src_ref=psend.at[s], dst_ref=pbuf.at[src], send_sem=c_ssem.at[s],
            recv_sem=c_rsem.at[src], device_id=dev(z, xl, y, xt, ct), device_id_type=MESH).wait_recv()
        total = total + pbuf[src].astype(F32)
    square = jnp.sum(jnp.sum(total * total, axis=2, keepdims=True), axis=1, keepdims=True)
    unit = (total * lax.rsqrt(square * (1.0 / 4096) + 1e-6)).astype(BF16)
    usend[0] = unit[:, :16]
    usend[1] = unit[:, 16:]

    me = z * 2 + core

    def send_u(i):
        z_, c_ = z_peers[i]
        return pltpu.make_async_remote_copy(
            src_ref=usend.at[c_], dst_ref=ubuf.at[me], send_sem=e_ssem.at[i], recv_sem=e_rsem.at[me],
            device_id=dev(z_, xl, y, xh, c_), device_id_type=MESH)

    for i in range(7):
        send_u(i).start()
    ubuf[me] = usend[core]

    for slot_y in range(4):
        for h in range(2):
            wait_q((1 - xl) * 4 + slot_y, h)
    for z_, c_ in z_peers:
        o = z_ * 2 + c_
        pltpu.make_async_remote_copy(
            src_ref=usend.at[0], dst_ref=ubuf.at[o], send_sem=e_ssem.at[0], recv_sem=e_rsem.at[o],
            device_id=dev(z_, xl, y, xh, c_), device_id_type=MESH).wait_recv()
    uf[...] = ubuf[...].astype(F32).reshape(512, 128)
    left = jnp.concatenate(
        [uf[pl.ds(r, 32, stride=16), :].astype(BF16) for r in range(16)], axis=1)
    scores = lax.dot_general(left, qbuf[...].reshape(512, 2048), NT, preferred_element_type=F32)
    for o in range(8):
        ssend[o] = scores[4 * o:4 * o + 4]

    def send_s(i):
        z_, c_ = z_peers[i]
        return pltpu.make_async_remote_copy(
            src_ref=ssend.at[z_ * 2 + c_], dst_ref=sbuf.at[me], send_sem=s_ssem.at[i],
            recv_sem=s_rsem.at[me], device_id=dev(z_, xl, y, xh, c_), device_id_type=MESH)

    for i in range(7):
        send_s(i).start()
    sbuf[me] = ssend[me]
    for i in range(3):
        send_part(i).wait_send()
    for i, (slot, h, to) in enumerate(q_sends):
        pltpu.make_async_remote_copy(
            src_ref=piece(slot, h), dst_ref=piece(slot, h), send_sem=q_ssem.at[i],
            recv_sem=q_rsem.at[slot, h], device_id=to, device_id_type=MESH).wait_send()
    for i in range(7):
        send_u(i).wait_send()
    for z_, c_ in z_peers:
        o = z_ * 2 + c_
        pltpu.make_async_remote_copy(
            src_ref=ssend.at[0], dst_ref=sbuf.at[o], send_sem=s_ssem.at[0], recv_sem=s_rsem.at[o],
            device_id=dev(z_, xl, y, xh, c_), device_id_type=MESH).wait_recv()
    for z_ in range(4):
        out[:, z_ * 512:(z_ + 1) * 512] = sbuf[2 * z_] + sbuf[2 * z_ + 1]
    for i in range(7):
        send_s(i).wait_send()


def on_device(acts, out_grads, proj_in, proj_out, lengths, queries):
    any_space = pl.BlockSpec(memory_space=pltpu.HBM)
    dma = pltpu.SemaphoreType.DMA
    return pl.pallas_call(
        kernel,
        name="scores",
        out_shape=jax.ShapeDtypeStruct((4, 2048), F32),
        in_specs=[pl.BlockSpec(memory_space=pltpu.SMEM)] + [any_space] * 5,
        out_specs=pl.BlockSpec(memory_space=pltpu.VMEM),
        scratch_shapes=[
            pltpu.VMEM((16, TOK, D), BF16),
            pltpu.VMEM((16, TOK, D), BF16),
            pltpu.VMEM((PR, D), BF16),
            pltpu.VMEM((PR, D), BF16),
            pltpu.VMEM((2, PR, PR), F32),
            pltpu.VMEM((4, 32, 128), F32),
            pltpu.VMEM((4, 4, 32, 128), BF16),
            pltpu.VMEM((4, 4, 32, 128), BF16),
            pltpu.VMEM((2, 4, 16, 128), BF16),
            pltpu.VMEM((8, 4, 16, 128), BF16),
            pltpu.VMEM((512, 128), F32),
            pltpu.VMEM((8, 64, 2048), BF16),
            pltpu.VMEM((8, 4, 512), F32),
            pltpu.VMEM((8, 4, 512), F32),
            dma((CHUNKS, 2)), dma((3,)), dma((14,)), dma((8, 2)), dma((3,)), dma((4,)),
            dma((7,)), dma((8,)), dma((7,)), dma((8,)),
        ],
        compiler_params=pltpu.CompilerParams(
            collective_id=0, has_side_effects=True, vmem_limit_bytes=62 * 2**20),
    )(lengths, acts[0], out_grads[0], proj_in[0].T, proj_out[0].T, queries)


def solution(mesh):
    in_specs = (
        P(None, "blk", "grp", None),
        P(None, "blk", "grp", None),
        P(),
        P(),
        P("blk"),
        P("blk", None),
    )
    return jax.shard_map(
        on_device, mesh=mesh, in_specs=in_specs, out_specs=P(("blk", "grp"), None), check_vma=False
    )
```

time: 226 us -> 32.5 us (0.14)
  the two profiles are of different devices: /device:TPU:0 before, /device:TPU:1 now
where the time goes in v1:
time: 32.5 us; the launch traced here: 32.3 us
  Pallas kernels  31 us (95%)
  local copies, waits for them, and re-layouts  1.38 us (4%)
    pallas_call x1, Pallas kernels, on_device(): pl.pallas_call(kernel, name='scores', out_shape=jax.ShapeDtypeStruct((4,...  31 us
    unnamed x1, local copies, waits for them, and re-layouts  1.38 us

profile of v1, /device:TPU:1, one launch (start us, length us, event | category | flops | bytes accessed | tf_op | source)
XLA Modules:
  0.0 32.3 jit_solution(16498017730396642420)
XLA Ops:
  0.0 31.0 %scores.1 = f32[4,2048]{1,0:T(4,128)} custom-call(s32[16]{0:T(128)} %lens.1, bf16[16,64,4096]{2,1,0:T(8,128)(2,1)} %bitcast.8, bf16[16,64,4096]{2,1,0:T(8,128)(2,1)} %bitcast.9, bf16[64,4096]{1,0:T(8,128)(2,1)} %bitcast.10, bf16[64,4096]{1,0:T(8,128)(2,1)} %bitcast.11, bf16[64,4096]{1,0:T(8,128)(2,1)} %q.1), custom_call_target="tpu_custom_call" | custom-call | tf_op jit(solution)/shard_map/scores/pallas_call | solution.py:224
  31.0 1.4 %copy.8 = f32[4,2048]{1,0:T(4,128)} copy(f32[4,2048]{1,0:T(4,128)} %scores.1) | data formatting | bytes 65536

commit v2 on v1

v2 whole, which is shorter than its diff:
```python
import functools

import jax
import jax.numpy as jnp
from jax import lax
from jax.experimental import pallas as pl
from jax.experimental.pallas import tpu as pltpu
from jax.sharding import PartitionSpec as P

MESH = pl.DeviceIdType.MESH
BF16, F32 = jnp.bfloat16, jnp.float32
D, PR, TOK = 4096, 64, 64
NT = (((1,), (1,)), ((), ()))
TN = (((0,), (0,)), ((), ()))
CHUNKS, AHEAD = 8, 2


def kernel(lens, acts, og, wi, wo, q, out,
           abuf, gbuf, wib, wob, pscr, pown, psend, pbuf, usend, ubuf, uf, qbuf, ssend, sbuf,
           ld_sem, w_sem, q_ssem, q_rsem, c_ssem, c_rsem, e_ssem, e_rsem, s_ssem, s_rsem):
    b, g = lax.axis_index("blk"), lax.axis_index("grp")
    z, xl, y = b // 8, (b // 4) % 2, b % 4
    xh, core = g // 2, g % 2

    def dev(z_, xl_, y_, xh_, c_):
        return (z_ * 8 + xl_ * 4 + y_, xh_ * 2 + c_)

    y_peers = [dev(z, xl, (y + dy) % 4, xh, core) for dy in (2, 1, 3)]
    peers = [((z + dz) % 4, (xl + dx) % 2, (core + dc) % 2)
             for dz in (2, 1, 3, 0) for dx in (1, 0) for dc in (0, 1) if (dz, dx, dc) != (0, 0, 0)]

    def peer(i):
        z_, xl_, c_ = peers[i]
        return dev(z_, xl_, y, xh, c_), (z_ * 2 + xl_) * 2 + c_

    def target(s):
        return (xh + 1 - s // 2) % 2, (core + (s + 1) // 2) % 2

    barrier = pltpu.get_barrier_semaphore()
    partners = y_peers + [peer(i)[0] for i in range(15)]
    partners += [dev(z, xl, y, *target(s)) for s in range(2)]
    for p in partners:
        pl.semaphore_signal(barrier, inc=1, device_id=p, device_id_type=MESH)

    def load(k):
        xt, ct = target(k // 2)
        first = (xt * 2 + ct) * 4 + (k % 2) * 2
        src = pl.ds(first, 2)
        return (pltpu.make_async_copy(acts.at[src], abuf.at[pl.ds(2 * k, 2)], ld_sem.at[k, 0]),
                pltpu.make_async_copy(og.at[src], gbuf.at[pl.ds(2 * k, 2)], ld_sem.at[k, 1]))

    w_loads = [pltpu.make_async_copy(wi, wib, w_sem.at[0]),
               pltpu.make_async_copy(wo, wob, w_sem.at[1])]
    q_load = pltpu.make_async_copy(
        q.at[:, pl.ds(pl.multiple_of(core * 2048, 2048), 2048)], qbuf.at[y], w_sem.at[2])
    for c in w_loads:
        c.start(priority=1)
    for k in range(AHEAD):
        for c in load(k):
            c.start(priority=1)
    q_load.start(priority=1)

    def send_q(i):
        return pltpu.make_async_remote_copy(
            src_ref=qbuf.at[y], dst_ref=qbuf.at[y], send_sem=q_ssem.at[i], recv_sem=q_rsem.at[y],
            device_id=y_peers[i], device_id_type=MESH)

    for c in w_loads:
        c.wait()
    pos = lax.broadcasted_iota(jnp.int32, (TOK, PR), 0) + g * TOK

    def chunk(k):
        for c in load(k):
            c.wait()

        @pl.when(k + AHEAD < CHUNKS)
        def _():
            for c in load(k + AHEAD):
                c.start(priority=1)

        s = k // 2
        xt, ct = target(s)
        first = (xt * 2 + ct) * 4 + (k % 2) * 2
        x = abuf[pl.ds(2 * k, 2)].reshape(2 * TOK, D)
        gr = gbuf[pl.ds(2 * k, 2)].reshape(2 * TOK, D)
        xp = lax.dot_general(x, wib[...], NT, preferred_element_type=F32).astype(BF16)
        gp = lax.dot_general(gr, wob[...], NT, preferred_element_type=F32)
        for i in range(2):
            rows = slice(i * TOK, (i + 1) * TOK)
            masked = jnp.where(pos < lens[first + i], gp[rows], 0.0).astype(BF16)
            pscr[i] = lax.dot_general(masked, xp[rows], TN, preferred_element_type=F32)
            part = jnp.concatenate(
                [pscr[i, pl.ds(0, 32, stride=2), :], pscr[i, pl.ds(1, 32, stride=2), :]], axis=1)
            pown[(k % 2) * 2 + i] = part
            psend[s, (k % 2) * 2 + i] = part.astype(BF16)

    def send_part(s):
        return pltpu.make_async_remote_copy(
            src_ref=psend.at[s], dst_ref=pbuf.at[g], send_sem=c_ssem.at[s], recv_sem=c_rsem.at[g],
            device_id=dev(z, xl, y, *target(s)), device_id_type=MESH)

    def run(first, last):
        def body(k, carry):
            chunk(k)
            return carry
        lax.fori_loop(first, last, body, 0)

    run(0, 1)
    q_load.wait()
    pl.semaphore_wait(barrier, len(partners))
    for i in range(3):
        send_q(i).start()
    run(1, 2)
    send_part(0).start()
    run(2, 4)
    send_part(1).start()
    run(4, 6)
    send_part(2).start()
    run(6, 8)

    total = pown[...]
    for s in range(3):
        xt, ct = target(s)
        src = xt * 2 + ct
        pltpu.make_async_remote_copy(
            src_ref=psend.at[s], dst_ref=pbuf.at[src], send_sem=c_ssem.at[s],
            recv_sem=c_rsem.at[src], device_id=dev(z, xl, y, xt, ct), device_id_type=MESH).wait_recv()
        total = total + pbuf[src].astype(F32)
    square = jnp.sum(jnp.sum(total * total, axis=2, keepdims=True), axis=1, keepdims=True)
    unit = (total * lax.rsqrt(square * (1.0 / 4096) + 1e-6)).astype(BF16)
    usend[0] = unit[:, :16]
    usend[1] = unit[:, 16:]

    me = (z * 2 + xl) * 2 + core

    def send_u(i):
        return pltpu.make_async_remote_copy(
            src_ref=usend.at[peers[i][2]], dst_ref=ubuf.at[me], send_sem=e_ssem.at[i],
            recv_sem=e_rsem.at[me], device_id=peer(i)[0], device_id_type=MESH)

    for i in range(15):
        send_u(i).start()
    ubuf[me] = usend[core]

    for i, dy in enumerate((2, 1, 3)):
        slot = (y + dy) % 4
        pltpu.make_async_remote_copy(
            src_ref=qbuf.at[slot], dst_ref=qbuf.at[slot], send_sem=q_ssem.at[i],
            recv_sem=q_rsem.at[slot], device_id=y_peers[i], device_id_type=MESH).wait_recv()
    for i in range(15):
        to, o = peer(i)
        pltpu.make_async_remote_copy(
            src_ref=usend.at[0], dst_ref=ubuf.at[o], send_sem=e_ssem.at[i], recv_sem=e_rsem.at[o],
            device_id=to, device_id_type=MESH).wait_recv()
    uf[...] = ubuf[...].astype(F32).reshape(1024, 128)
    left = jnp.concatenate(
        [uf[pl.ds(r, 64, stride=16), :].astype(BF16) for r in range(16)], axis=1)
    scores = lax.dot_general(left, qbuf[...].reshape(256, 2048), NT, preferred_element_type=F32)
    for o in range(16):
        ssend[o] = scores[4 * o:4 * o + 4]

    def send_s(i):
        to, o = peer(i)
        return pltpu.make_async_remote_copy(
            src_ref=ssend.at[o], dst_ref=sbuf.at[me], send_sem=s_ssem.at[i],
            recv_sem=s_rsem.at[me], device_id=to, device_id_type=MESH)

    for i in range(15):
        send_s(i).start()
    sbuf[me] = ssend[me]
    for i in range(3):
        send_part(i).wait_send()
        send_q(i).wait_send()
    for i in range(15):
        send_u(i).wait_send()
    for i in range(15):
        to, o = peer(i)
        pltpu.make_async_remote_copy(
            src_ref=ssend.at[0], dst_ref=sbuf.at[o], send_sem=s_ssem.at[i], recv_sem=s_rsem.at[o],
            device_id=to, device_id_type=MESH).wait_recv()
    for o in range(8):
        out[:, o * 256:(o + 1) * 256] = sbuf[2 * o] + sbuf[2 * o + 1]
    for i in range(15):
        send_s(i).wait_send()


def on_device(acts, out_grads, proj_in, proj_out, lengths, queries):
    any_space = pl.BlockSpec(memory_space=pltpu.HBM)
    dma = pltpu.SemaphoreType.DMA
    return pl.pallas_call(
        kernel,
        name="scores",
        out_shape=jax.ShapeDtypeStruct((4, 2048), F32),
        in_specs=[pl.BlockSpec(memory_space=pltpu.SMEM)] + [any_space] * 5,
        out_specs=pl.BlockSpec(memory_space=pltpu.VMEM),
        scratch_shapes=[
            pltpu.VMEM((16, TOK, D), BF16),
            pltpu.VMEM((16, TOK, D), BF16),
            pltpu.VMEM((PR, D), BF16),
            pltpu.VMEM((PR, D), BF16),
            pltpu.VMEM((2, PR, PR), F32),
            pltpu.VMEM((4, 32, 128), F32),
            pltpu.VMEM((4, 4, 32, 128), BF16),
            pltpu.VMEM((4, 4, 32, 128), BF16),
            pltpu.VMEM((2, 4, 16, 128), BF16),
            pltpu.VMEM((16, 4, 16, 128), BF16),
            pltpu.VMEM((1024, 128), F32),
            pltpu.VMEM((4, 64, 2048), BF16),
            pltpu.VMEM((16, 4, 256), F32),
            pltpu.VMEM((16, 4, 256), F32),
            dma((CHUNKS, 2)), dma((3,)), dma((3,)), dma((4,)), dma((3,)), dma((4,)),
            dma((15,)), dma((16,)), dma((15,)), dma((16,)),
        ],
        compiler_params=pltpu.CompilerParams(
            collective_id=0, has_side_effects=True, vmem_limit_bytes=62 * 2**20),
    )(lengths, acts[0], out_grads[0], proj_in[0].T, proj_out[0].T, queries)


def solution(mesh):
    in_specs = (
        P(None, "blk", "grp", None),
        P(None, "blk", "grp", None),
        P(),
        P(),
        P("blk"),
        P("blk", None),
    )
    return jax.shard_map(
        on_device, mesh=mesh, in_specs=in_specs, out_specs=P(("blk", "grp"), None), check_vma=False
    )
```

time: 32.5 us -> 29.9 us (0.920)
  Pallas kernels: 31 us -> 28.3 us
    pallas_call x1, Pallas kernels: 31 us -> 28.3 us  [on_device(): pl.pallas_call(kernel, name='scores', out_shape=jax.ShapeDtypeStruct((4,...]
where the time goes in v2:
time: 29.9 us; the launch traced here: 29.7 us
  Pallas kernels  28.3 us (95%)
  local copies, waits for them, and re-layouts  1.38 us (5%)
    pallas_call x1, Pallas kernels, on_device(): pl.pallas_call(kernel, name='scores', out_shape=jax.ShapeDtypeStruct((4,...  28.3 us
    unnamed x1, local copies, waits for them, and re-layouts  1.38 us

profile of v2, /device:TPU:1, one launch (start us, length us, event | category | flops | bytes accessed | tf_op | source)
XLA Modules:
  0.0 29.7 jit_solution(7852803669046662215)
XLA Ops:
  0.0 28.3 %scores.1 = f32[4,2048]{1,0:T(4,128)} custom-call(s32[16]{0:T(128)} %lens.1, bf16[16,64,4096]{2,1,0:T(8,128)(2,1)} %bitcast.8, bf16[16,64,4096]{2,1,0:T(8,128)(2,1)} %bitcast.9, bf16[64,4096]{1,0:T(8,128)(2,1)} %bitcast.10, bf16[64,4096]{1,0:T(8,128)(2,1)} %bitcast.11, bf16[64,4096]{1,0:T(8,128)(2,1)} %q.1), custom_call_target="tpu_custom_call" | custom-call | tf_op jit(solution)/shard_map/scores/pallas_call | solution.py:190
  28.3 1.4 %copy.8 = f32[4,2048]{1,0:T(4,128)} copy(f32[4,2048]{1,0:T(4,128)} %scores.1) | data formatting | bytes 65536

commit v3 on v2

v3 whole, which is shorter than its diff:
```python
import functools

import jax
import jax.numpy as jnp
from jax import lax
from jax.experimental import pallas as pl
from jax.experimental.pallas import tpu as pltpu
from jax.sharding import PartitionSpec as P

MESH = pl.DeviceIdType.MESH
BF16, F32 = jnp.bfloat16, jnp.float32
D, PR, TOK = 4096, 64, 64
NT = (((1,), (1,)), ((), ()))
TN = (((0,), (0,)), ((), ()))
COLS, AHEAD = 2048, 2
SPLIT = D // COLS
PIECES = 4 * SPLIT
FORWARD = 6


def kernel(lens_hbm, acts, og, wi, wo, q, out,
           abuf, gbuf, wib, wob, xacc, gacc, pscr, pown, psend, pbuf, usend, ubuf, uf, qbuf, ssend, sbuf,
           lens, ld_sem, w_sem, q_ssem, q_rsem, c_ssem, c_rsem, e_ssem, e_rsem, s_ssem, s_rsem):
    b, g = lax.axis_index("blk"), lax.axis_index("grp")
    z, xl, y = b // 8, (b // 4) % 2, b % 4
    xh, core = g // 2, g % 2

    def dev(z_, xl_, y_, xh_, c_):
        return (z_ * 8 + xl_ * 4 + y_, xh_ * 2 + c_)

    up, down, far = (y + 1) % 4, (y + 3) % 4, (y + 2) % 4
    y_up, y_down = dev(z, xl, up, xh, core), dev(z, xl, down, xh, core)
    peers = [((z + dz) % 4, (xl + dx) % 2, (core + dc) % 2)
             for dz in (2, 1, 3, 0) for dx in (1, 0) for dc in (0, 1) if (dz, dx, dc) != (0, 0, 0)]

    def peer(i):
        z_, xl_, c_ = peers[i]
        return dev(z_, xl_, y, xh, c_), (z_ * 2 + xl_) * 2 + c_

    def target(s):
        return (xh + 1 - s // 2) % 2, (core + (s + 1) // 2) % 2

    barrier = pltpu.get_barrier_semaphore()
    partners = [y_up, y_down] + [peer(i)[0] for i in range(15)]
    partners += [dev(z, xl, y, *target(s)) for s in range(2)]
    for p in partners:
        pl.semaphore_signal(barrier, inc=1, device_id=p, device_id_type=MESH)

    def load(i):
        xt, ct = target(i // SPLIT)
        rows = pl.ds((xt * 2 + ct) * 4, 4)
        cols = pl.ds(pl.multiple_of((i % SPLIT) * COLS, COLS), COLS)
        return (pltpu.make_async_copy(acts.at[rows, :, cols], abuf.at[i], ld_sem.at[i, 0]),
                pltpu.make_async_copy(og.at[rows, :, cols], gbuf.at[i], ld_sem.at[i, 1]))

    w_loads = [pltpu.make_async_copy(wi, wib.at[pl.ds(0, PR)], w_sem.at[0]),
               pltpu.make_async_copy(wo, wob, w_sem.at[1])]
    q_load = pltpu.make_async_copy(
        q.at[:, pl.ds(pl.multiple_of(core * 2048, 2048), 2048)], qbuf.at[y], w_sem.at[2])
    for c in w_loads:
        c.start(priority=1)
    for k in range(AHEAD):
        for c in load(k):
            c.start(priority=1)
    q_load.start(priority=1)
    l_load = pltpu.make_async_copy(lens_hbm, lens, w_sem.at[3])
    l_load.start()

    q_moves = [(y, 0, y_up), (y, 1, y_down), (y, 1, y_up), (y, 0, y_down), (down, 0, y_up), (up, 1, y_down)]

    def move_q(i):
        slot, h, to = q_moves[i]
        half = qbuf.at[slot, pl.ds(h * 32, 32)]
        return pltpu.make_async_remote_copy(
            src_ref=half, dst_ref=half, send_sem=q_ssem.at[i], recv_sem=q_rsem.at[slot, h],
            device_id=to, device_id_type=MESH)

    def wait_q(slot, h):
        half = qbuf.at[slot, pl.ds(h * 32, 32)]
        pltpu.make_async_remote_copy(
            src_ref=half, dst_ref=half, send_sem=q_ssem.at[0], recv_sem=q_rsem.at[slot, h],
            device_id=y_up, device_id_type=MESH).wait_recv()

    def send_part(s):
        return pltpu.make_async_remote_copy(
            src_ref=psend.at[s], dst_ref=pbuf.at[g], send_sem=c_ssem.at[s], recv_sem=c_rsem.at[g],
            device_id=dev(z, xl, y, *target(s)), device_id_type=MESH)

    for c in w_loads:
        c.wait()
    l_load.wait()
    wib[pl.ds(PR, PR)] = wib[pl.ds(0, PR)]
    pos = lax.broadcasted_iota(jnp.int32, (TOK, PR), 0) + g * TOK
    low = lax.broadcasted_iota(jnp.int32, (32, 128), 1) < PR

    def step(i, carry):
        s, k = i // SPLIT, i % SPLIT
        for c in load(i):
            c.wait()

        @pl.when(i + AHEAD < PIECES)
        def _():
            for c in load(i + AHEAD):
                c.start(priority=1)

        cols = pl.ds(pl.multiple_of(k * COLS, COLS), COLS)
        xp = lax.dot_general(
            abuf[i].reshape(4 * TOK, COLS), wib[:, cols], NT, preferred_element_type=F32)
        gp = lax.dot_general(
            gbuf[i].reshape(4 * TOK, COLS), wob[:, cols], NT, preferred_element_type=F32)

        @pl.when(k == 0)
        def _():
            xacc[...] = xp
            gacc[...] = gp

        @pl.when(k > 0)
        def _():
            xacc[...] += xp
            gacc[...] += gp

        @pl.when(i == 0)
        def _():
            q_load.wait()
            pl.semaphore_wait(barrier, len(partners))
            for j in range(4):
                move_q(j).start()

        @pl.when(k == SPLIT - 1)
        def _():
            xt, ct = target(s)
            for c in range(4):
                rows = pl.ds(c * TOK, TOK)
                left = jnp.where(pos < lens[(xt * 2 + ct) * 4 + c], gacc[rows], 0.0).astype(BF16)
                pscr[c] = lax.dot_general(
                    left, xacc[rows].astype(BF16), TN, preferred_element_type=F32)
                part = jnp.where(
                    low, pscr[c, pl.ds(0, 32, stride=2), :], pscr[c, pl.ds(1, 32, stride=2), :])
                pown[c] = part
                psend[s, c] = part.astype(BF16)

        @pl.when(jnp.logical_and(k == SPLIT - 1, s < 3))
        def _():
            send_part(s).start()

        @pl.when(i == FORWARD)
        def _():
            wait_q(down, 0)
            move_q(4).start()
            wait_q(up, 1)
            move_q(5).start()

        return carry

    lax.fori_loop(0, PIECES, step, 0)

    total = pown[...]
    for s in range(3):
        xt, ct = target(s)
        src = xt * 2 + ct
        pltpu.make_async_remote_copy(
            src_ref=psend.at[s], dst_ref=pbuf.at[src], send_sem=c_ssem.at[s],
            recv_sem=c_rsem.at[src], device_id=dev(z, xl, y, xt, ct), device_id_type=MESH).wait_recv()
        total = total + pbuf[src].astype(F32)
    square = jnp.sum(jnp.sum(total * total, axis=2, keepdims=True), axis=1, keepdims=True)
    unit = (total * lax.rsqrt(square * (1.0 / 4096) + 1e-6)).astype(BF16)
    usend[0] = unit[:, :16]
    usend[1] = unit[:, 16:]

    me = (z * 2 + xl) * 2 + core

    def send_u(i):
        return pltpu.make_async_remote_copy(
            src_ref=usend.at[peers[i][2]], dst_ref=ubuf.at[me], send_sem=e_ssem.at[i],
            recv_sem=e_rsem.at[me], device_id=peer(i)[0], device_id_type=MESH)

    for i in range(15):
        send_u(i).start()
    ubuf[me] = usend[core]

    for slot, h in ((down, 1), (up, 0), (far, 0), (far, 1)):
        wait_q(slot, h)
    for i in range(15):
        to, o = peer(i)
        pltpu.make_async_remote_copy(
            src_ref=usend.at[0], dst_ref=ubuf.at[o], send_sem=e_ssem.at[i], recv_sem=e_rsem.at[o],
            device_id=to, device_id_type=MESH).wait_recv()
    uf[...] = ubuf[...].astype(F32).reshape(1024, 128)
    left = jnp.concatenate(
        [uf[pl.ds(r, 64, stride=16), :].astype(BF16) for r in range(16)], axis=1)
    scores = lax.dot_general(left, qbuf[...].reshape(256, 2048), NT, preferred_element_type=F32)
    for o in range(16):
        ssend[o] = scores[4 * o:4 * o + 4]

    def send_s(i):
        to, o = peer(i)
        return pltpu.make_async_remote_copy(
            src_ref=ssend.at[o], dst_ref=sbuf.at[me], send_sem=s_ssem.at[i],
            recv_sem=s_rsem.at[me], device_id=to, device_id_type=MESH)

    for i in range(15):
        send_s(i).start()
    sbuf[me] = ssend[me]
    for i in range(3):
        send_part(i).wait_send()
    for i in range(6):
        move_q(i).wait_send()
    for i in range(15):
        send_u(i).wait_send()
    for i in range(15):
        to, o = peer(i)
        pltpu.make_async_remote_copy(
            src_ref=ssend.at[0], dst_ref=sbuf.at[o], send_sem=s_ssem.at[i], recv_sem=s_rsem.at[o],
            device_id=to, device_id_type=MESH).wait_recv()
    for o in range(8):
        out[:, o * 256:(o + 1) * 256] = sbuf[2 * o] + sbuf[2 * o + 1]
    for i in range(15):
        send_s(i).wait_send()


def on_device(acts, out_grads, proj_in, proj_out, lengths, queries):
    any_space = pl.BlockSpec(memory_space=pltpu.HBM)
    dma = pltpu.SemaphoreType.DMA
    return pl.pallas_call(
        kernel,
        name="scores",
        out_shape=pltpu.VMEM((4, 2048), F32),
        in_specs=[any_space] * 6,
        out_specs=pl.BlockSpec(memory_space=pltpu.VMEM),
        scratch_shapes=[
            pltpu.VMEM((PIECES, 4, TOK, COLS), BF16),
            pltpu.VMEM((PIECES, 4, TOK, COLS), BF16),
            pltpu.VMEM((2 * PR, D), BF16),
            pltpu.VMEM((PR, D), BF16),
            pltpu.VMEM((4 * TOK, 2 * PR), F32),
            pltpu.VMEM((4 * TOK, PR), F32),
            pltpu.VMEM((4, PR, 2 * PR), F32),
            pltpu.VMEM((4, 32, 128), F32),
            pltpu.VMEM((4, 4, 32, 128), BF16),
            pltpu.VMEM((4, 4, 32, 128), BF16),
            pltpu.VMEM((2, 4, 16, 128), BF16),
            pltpu.VMEM((16, 4, 16, 128), BF16),
            pltpu.VMEM((1024, 128), F32),
            pltpu.VMEM((4, 64, 2048), BF16),
            pltpu.VMEM((16, 4, 256), F32),
            pltpu.VMEM((16, 4, 256), F32),
            pltpu.SMEM((16,), jnp.int32), dma((PIECES, 2)), dma((4,)), dma((6,)), dma((4, 2)), dma((3,)), dma((4,)),
            dma((15,)), dma((16,)), dma((15,)), dma((16,)),
        ],
        compiler_params=pltpu.CompilerParams(
            collective_id=0, has_side_effects=True, vmem_limit_bytes=62*2**20),
    )(lengths, acts[0], out_grads[0], proj_in[0].T, proj_out[0].T, queries)


def solution(mesh):
    in_specs = (
        P(None, "blk", "grp", None),
        P(None, "blk", "grp", None),
        P(),
        P(),
        P("blk"),
        P("blk", None),
    )
    return jax.shard_map(
        on_device, mesh=mesh, in_specs=in_specs, out_specs=P(("blk", "grp"), None), check_vma=False
    )
```

time: 29.9 us -> 25.2 us (0.84)
  Pallas kernels: 28.3 us -> 24.4 us
  local copies, waits for them, and re-layouts: 1.38 us -> 0.62 us
    pallas_call x1, Pallas kernels: 28.3 us -> 24.4 us  [on_device(): pl.pallas_call(kernel, name='scores', out_shape=pltpu.VMEM((4, 2048), F32...]
    unnamed x1, local copies, waits for them, and re-layouts: 1.38 us -> 0.62 us
where the time goes in v3:
time: 25.2 us; the launch traced here: 25.1 us
  Pallas kernels  24.4 us (97%)
  local copies, waits for them, and re-layouts  0.62 us (2%)
    pallas_call x1, Pallas kernels, on_device(): pl.pallas_call(kernel, name='scores', out_shape=pltpu.VMEM((4, 2048), F32...  24.4 us
    unnamed x1, local copies, waits for them, and re-layouts  0.62 us

profile of v3, /device:TPU:1, one launch (start us, length us, event | category | flops | bytes accessed | tf_op | source)
XLA Modules:
  0.0 25.1 jit_solution(5503095840548902692)
XLA Ops:
  0.0 24.4 %scores.1 = f32[4,2048]{1,0:T(4,128)S(1)} custom-call(s32[16]{0:T(128)} %lens_hbm.1, bf16[16,64,4096]{2,1,0:T(8,128)(2,1)} %bitcast.8, bf16[16,64,4096]{2,1,0:T(8,128)(2,1)} %bitcast.9, bf16[64,4096]{1,0:T(8,128)(2,1)} %bitcast.10, bf16[64,4096]{1,0:T(8,128)(2,1)} %bitcast.11, bf16[64,4096]{1,0:T(8,128)(2,1)} %q.1), custom_call_target="tpu_custom_call" | custom-call | tf_op jit(solution)/shard_map/scores/pallas_call | solution.py:224
  24.4 0.6 %copy.8 = f32[4,2048]{1,0:T(4,128)} copy(f32[4,2048]{1,0:T(4,128)S(1)} %scores.1) | data formatting | bytes 65536

commit v4 on v3

--- a/solution.py
+++ b/solution.py
@@ -43,8 +43,6 @@
     barrier = pltpu.get_barrier_semaphore()
     partners = [y_up, y_down] + [peer(i)[0] for i in range(15)]
     partners += [dev(z, xl, y, *target(s)) for s in range(2)]
-    for p in partners:
-        pl.semaphore_signal(barrier, inc=1, device_id=p, device_id_type=MESH)
 
     def load(i):
         xt, ct = target(i // SPLIT)
@@ -57,12 +55,12 @@
                pltpu.make_async_copy(wo, wob, w_sem.at[1])]
     q_load = pltpu.make_async_copy(
         q.at[:, pl.ds(pl.multiple_of(core * 2048, 2048), 2048)], qbuf.at[y], w_sem.at[2])
-    for c in w_loads:
+    for c in (*w_loads, *load(0)):
         c.start(priority=1)
-    for k in range(AHEAD):
-        for c in load(k):
-            c.start(priority=1)
-    q_load.start(priority=1)
+    for p in partners:
+        pl.semaphore_signal(barrier, inc=1, device_id=p, device_id_type=MESH)
+    for c in (*load(1), q_load):
+        c.start(priority=1)
     l_load = pltpu.make_async_copy(lens_hbm, lens, w_sem.at[3])
     l_load.start()
 
@@ -162,8 +160,7 @@
             src_ref=psend.at[s], dst_ref=pbuf.at[src], send_sem=c_ssem.at[s],
             recv_sem=c_rsem.at[src], device_id=dev(z, xl, y, xt, ct), device_id_type=MESH).wait_recv()
         total = total + pbuf[src].astype(F32)
-    square = jnp.sum(jnp.sum(total * total, axis=2, keepdims=True), axis=1, keepdims=True)
-    unit = (total * lax.rsqrt(square * (1.0 / 4096) + 1e-6)).astype(BF16)
+    unit = total.astype(BF16)
     usend[0] = unit[:, :16]
     usend[1] = unit[:, 16:]
 
@@ -177,15 +174,21 @@
     for i in range(15):
         send_u(i).start()
     ubuf[me] = usend[core]
+    square = jnp.sum(jnp.sum(total * total, axis=2, keepdims=True), axis=1, keepdims=True)
+    scale = lax.rsqrt(square * (1.0 / 4096) + 1e-6)[:, :, 0]
 
     for slot, h in ((down, 1), (up, 0), (far, 0), (far, 1)):
         wait_q(slot, h)
-    for i in range(15):
+    def lay_out(o):
+        uf[pl.ds(pl.multiple_of(o * 64, 64), 64)] = ubuf[o].astype(F32).reshape(64, 128)
+
+    lay_out(me)
+    for i in reversed(range(15)):
         to, o = peer(i)
         pltpu.make_async_remote_copy(
             src_ref=usend.at[0], dst_ref=ubuf.at[o], send_sem=e_ssem.at[i], recv_sem=e_rsem.at[o],
             device_id=to, device_id_type=MESH).wait_recv()
-    uf[...] = ubuf[...].astype(F32).reshape(1024, 128)
+        lay_out(o)
     left = jnp.concatenate(
         [uf[pl.ds(r, 64, stride=16), :].astype(BF16) for r in range(16)], axis=1)
     scores = lax.dot_general(left, qbuf[...].reshape(256, 2048), NT, preferred_element_type=F32)
@@ -213,7 +216,7 @@
             src_ref=ssend.at[0], dst_ref=sbuf.at[o], send_sem=s_ssem.at[i], recv_sem=s_rsem.at[o],
             device_id=to, device_id_type=MESH).wait_recv()
     for o in range(8):
-        out[:, o * 256:(o + 1) * 256] = sbuf[2 * o] + sbuf[2 * o + 1]
+        out[:, o * 256:(o + 1) * 256] = (sbuf[2 * o] + sbuf[2 * o + 1]) * scale
     for i in range(15):
         send_s(i).wait_send()
 

time: 25.2 us -> 25.1 us (level)
  no operation moved by 1% of the time
where the time goes in v4:
time: 25.1 us; the launch traced here: 25 us
  Pallas kernels  24.4 us (97%)
  local copies, waits for them, and re-layouts  0.62 us (2%)
    pallas_call x1, Pallas kernels, on_device(): pl.pallas_call(kernel, name='scores', out_shape=pltpu.VMEM((4, 2048), F32...  24.4 us
    unnamed x1, local copies, waits for them, and re-layouts  0.62 us

profile of v4, /device:TPU:1, one launch (start us, length us, event | category | flops | bytes accessed | tf_op | source)
XLA Modules:
  0.0 25.0 jit_solution(14896904719591629366)
XLA Ops:
  0.0 24.4 %scores.1 = f32[4,2048]{1,0:T(4,128)S(1)} custom-call(s32[16]{0:T(128)} %lens_hbm.1, bf16[16,64,4096]{2,1,0:T(8,128)(2,1)} %bitcast.8, bf16[16,64,4096]{2,1,0:T(8,128)(2,1)} %bitcast.9, bf16[64,4096]{1,0:T(8,128)(2,1)} %bitcast.10, bf16[64,4096]{1,0:T(8,128)(2,1)} %bitcast.11, bf16[64,4096]{1,0:T(8,128)(2,1)} %q.1), custom_call_target="tpu_custom_call" | custom-call | tf_op jit(solution)/shard_map/scores/pallas_call | solution.py:227
  24.4 0.6 %copy.8 = f32[4,2048]{1,0:T(4,128)} copy(f32[4,2048]{1,0:T(4,128)S(1)} %scores.1) | data formatting | bytes 65536

commit v5 on v3

--- a/solution.py
+++ b/solution.py
@@ -172,7 +172,7 @@
     def send_u(i):
         return pltpu.make_async_remote_copy(
             src_ref=usend.at[peers[i][2]], dst_ref=ubuf.at[me], send_sem=e_ssem.at[i],
-            recv_sem=e_rsem.at[me], device_id=peer(i)[0], device_id_type=MESH)
+            recv_sem=e_rsem.at[0], device_id=peer(i)[0], device_id_type=MESH)
 
     for i in range(15):
         send_u(i).start()
@@ -180,11 +180,10 @@
 
     for slot, h in ((down, 1), (up, 0), (far, 0), (far, 1)):
         wait_q(slot, h)
-    for i in range(15):
-        to, o = peer(i)
-        pltpu.make_async_remote_copy(
-            src_ref=usend.at[0], dst_ref=ubuf.at[o], send_sem=e_ssem.at[i], recv_sem=e_rsem.at[o],
-            device_id=to, device_id_type=MESH).wait_recv()
+    fifteen = pl.ds(0, 15)
+    pltpu.make_async_remote_copy(
+        src_ref=ubuf.at[fifteen], dst_ref=ubuf.at[fifteen], send_sem=e_ssem.at[0],
+        recv_sem=e_rsem.at[0], device_id=peer(0)[0], device_id_type=MESH).wait_recv()
     uf[...] = ubuf[...].astype(F32).reshape(1024, 128)
     left = jnp.concatenate(
         [uf[pl.ds(r, 64, stride=16), :].astype(BF16) for r in range(16)], axis=1)
@@ -196,7 +195,7 @@
         to, o = peer(i)
         return pltpu.make_async_remote_copy(
             src_ref=ssend.at[o], dst_ref=sbuf.at[me], send_sem=s_ssem.at[i],
-            recv_sem=s_rsem.at[me], device_id=to, device_id_type=MESH)
+            recv_sem=s_rsem.at[0], device_id=to, device_id_type=MESH)
 
     for i in range(15):
         send_s(i).start()
@@ -207,11 +206,9 @@
         move_q(i).wait_send()
     for i in range(15):
         send_u(i).wait_send()
-    for i in range(15):
-        to, o = peer(i)
-        pltpu.make_async_remote_copy(
-            src_ref=ssend.at[0], dst_ref=sbuf.at[o], send_sem=s_ssem.at[i], recv_sem=s_rsem.at[o],
-            device_id=to, device_id_type=MESH).wait_recv()
+    pltpu.make_async_remote_copy(
+        src_ref=sbuf.at[fifteen], dst_ref=sbuf.at[fifteen], send_sem=s_ssem.at[0],
+        recv_sem=s_rsem.at[0], device_id=peer(0)[0], device_id_type=MESH).wait_recv()
     for o in range(8):
         out[:, o * 256:(o + 1) * 256] = sbuf[2 * o] + sbuf[2 * o + 1]
     for i in range(15):
@@ -245,7 +242,7 @@
             pltpu.VMEM((16, 4, 256), F32),
             pltpu.VMEM((16, 4, 256), F32),
             pltpu.SMEM((16,), jnp.int32), dma((PIECES, 2)), dma((4,)), dma((6,)), dma((4, 2)), dma((3,)), dma((4,)),
-            dma((15,)), dma((16,)), dma((15,)), dma((16,)),
+            dma((15,)), dma((1,)), dma((15,)), dma((1,)),
         ],
         compiler_params=pltpu.CompilerParams(
             collective_id=0, has_side_effects=True, vmem_limit_bytes=62*2**20),

time: 25.2 us -> 24.9 us (0.988)
  Pallas kernels: 24.4 us -> 24.1 us
    pallas_call x1, Pallas kernels: 24.4 us -> 24.1 us  [on_device(): pl.pallas_call(kernel, name='scores', out_shape=pltpu.VMEM((4, 2048), F32...]
where the time goes in v5:
time: 24.9 us; the launch traced here: 24.8 us
  Pallas kernels  24.1 us (97%)
  local copies, waits for them, and re-layouts  0.62 us (2%)
    pallas_call x1, Pallas kernels, on_device(): pl.pallas_call(kernel, name='scores', out_shape=pltpu.VMEM((4, 2048), F32...  24.1 us
    unnamed x1, local copies, waits for them, and re-layouts  0.62 us

profile of v5, /device:TPU:1, one launch (start us, length us, event | category | flops | bytes accessed | tf_op | source)
XLA Modules:
  0.0 24.8 jit_solution(1597726886621156217)
XLA Ops:
  0.0 24.1 %scores.1 = f32[4,2048]{1,0:T(4,128)S(1)} custom-call(s32[16]{0:T(128)} %lens_hbm.1, bf16[16,64,4096]{2,1,0:T(8,128)(2,1)} %bitcast.8, bf16[16,64,4096]{2,1,0:T(8,128)(2,1)} %bitcast.9, bf16[64,4096]{1,0:T(8,128)(2,1)} %bitcast.10, bf16[64,4096]{1,0:T(8,128)(2,1)} %bitcast.11, bf16[64,4096]{1,0:T(8,128)(2,1)} %q.1), custom_call_target="tpu_custom_call" | custom-call | tf_op jit(solution)/shard_map/scores/pallas_call | solution.py:221
  24.1 0.6 %copy.8 = f32[4,2048]{1,0:T(4,128)} copy(f32[4,2048]{1,0:T(4,128)S(1)} %scores.1) | data formatting | bytes 65536

commit v6 on v5

--- a/solution.py
+++ b/solution.py
@@ -171,7 +171,7 @@
 
     def send_u(i):
         return pltpu.make_async_remote_copy(
-            src_ref=usend.at[peers[i][2]], dst_ref=ubuf.at[me], send_sem=e_ssem.at[i],
+            src_ref=usend.at[peers[i][2]], dst_ref=ubuf.at[me], send_sem=e_ssem.at[0],
             recv_sem=e_rsem.at[0], device_id=peer(i)[0], device_id_type=MESH)
 
     for i in range(15):
@@ -194,7 +194,7 @@
     def send_s(i):
         to, o = peer(i)
         return pltpu.make_async_remote_copy(
-            src_ref=ssend.at[o], dst_ref=sbuf.at[me], send_sem=s_ssem.at[i],
+            src_ref=ssend.at[o], dst_ref=sbuf.at[me], send_sem=s_ssem.at[0],
             recv_sem=s_rsem.at[0], device_id=to, device_id_type=MESH)
 
     for i in range(15):
@@ -204,15 +204,17 @@
         send_part(i).wait_send()
     for i in range(6):
         move_q(i).wait_send()
-    for i in range(15):
-        send_u(i).wait_send()
+    pltpu.make_async_remote_copy(
+        src_ref=ubuf.at[fifteen], dst_ref=ubuf.at[fifteen], send_sem=e_ssem.at[0],
+        recv_sem=e_rsem.at[0], device_id=peer(0)[0], device_id_type=MESH).wait_send()
     pltpu.make_async_remote_copy(
         src_ref=sbuf.at[fifteen], dst_ref=sbuf.at[fifteen], send_sem=s_ssem.at[0],
         recv_sem=s_rsem.at[0], device_id=peer(0)[0], device_id_type=MESH).wait_recv()
     for o in range(8):
         out[:, o * 256:(o + 1) * 256] = sbuf[2 * o] + sbuf[2 * o + 1]
-    for i in range(15):
-        send_s(i).wait_send()
+    pltpu.make_async_remote_copy(
+        src_ref=ssend.at[fifteen], dst_ref=sbuf.at[fifteen], send_sem=s_ssem.at[0],
+        recv_sem=s_rsem.at[0], device_id=peer(0)[0], device_id_type=MESH).wait_send()
 
 
 def on_device(acts, out_grads, proj_in, proj_out, lengths, queries):
@@ -242,7 +244,7 @@
             pltpu.VMEM((16, 4, 256), F32),
             pltpu.VMEM((16, 4, 256), F32),
             pltpu.SMEM((16,), jnp.int32), dma((PIECES, 2)), dma((4,)), dma((6,)), dma((4, 2)), dma((3,)), dma((4,)),
-            dma((15,)), dma((1,)), dma((15,)), dma((1,)),
+            dma((1,)), dma((1,)), dma((1,)), dma((1,)),
         ],
         compiler_params=pltpu.CompilerParams(
             collective_id=0, has_side_effects=True, vmem_limit_bytes=62*2**20),

time: 24.9 us -> 24.6 us (0.988)
    pallas_call x1, Pallas kernels: 24.1 us -> 23.9 us  [on_device(): pl.pallas_call(kernel, name='scores', out_shape=pltpu.VMEM((4, 2048), F32...]
where the time goes in v6:
time: 24.6 us; the launch traced here: 24.5 us
  Pallas kernels  23.9 us (97%)
  local copies, waits for them, and re-layouts  0.62 us (3%)
    pallas_call x1, Pallas kernels, on_device(): pl.pallas_call(kernel, name='scores', out_shape=pltpu.VMEM((4, 2048), F32...  23.9 us
    unnamed x1, local copies, waits for them, and re-layouts  0.62 us

profile of v6, /device:TPU:1, one launch (start us, length us, event | category | flops | bytes accessed | tf_op | source)
XLA Modules:
  0.0 24.5 jit_solution(11483977258496310808)
XLA Ops:
  0.0 23.9 %scores.1 = f32[4,2048]{1,0:T(4,128)S(1)} custom-call(s32[16]{0:T(128)} %lens_hbm.1, bf16[16,64,4096]{2,1,0:T(8,128)(2,1)} %bitcast.8, bf16[16,64,4096]{2,1,0:T(8,128)(2,1)} %bitcast.9, bf16[64,4096]{1,0:T(8,128)(2,1)} %bitcast.10, bf16[64,4096]{1,0:T(8,128)(2,1)} %bitcast.11, bf16[64,4096]{1,0:T(8,128)(2,1)} %q.1), custom_call_target="tpu_custom_call" | custom-call | tf_op jit(solution)/shard_map/scores/pallas_call | solution.py:223
  23.9 0.6 %copy.8 = f32[4,2048]{1,0:T(4,128)} copy(f32[4,2048]{1,0:T(4,128)S(1)} %scores.1) | data formatting | bytes 65536
